TPU v7x, 32 devices: a whole 2x2x4 slice. The times are simulated.
32 devices in a mesh: wide: 16 (over z, y, x), narrow: 2 (over core).
Axes of the slice: x: 2, y: 2, z: 4, core: 2. Of those that a mesh axis runs over, the one named last changes fastest.
Arguments:
- filt_mean: float32 [128, 128], P(('wide', 'narrow')), may hold values from -6 to 6
- filtered_covariance: float32 [128, 128, 128], P(('wide', 'narrow')), may hold values from -9 to 13, as said below
- noise_cov: float32 [128, 128], replicated, may hold values from -1 to 2, as said below
Outputs:
- smooth_mean: float32 [128, 128], P(('wide', 'narrow'))
- smooth_cov: float32 [128, 128, 128], P(('wide', 'narrow'))
- increment_var: float32 [128, 128], P(('wide', 'narrow'))
Inputs may be any that keep to these rules, and one draw needn't show every extreme that they name: `filtered_covariance`: each 128 x 128 slice is symmetric positive definite. `noise_cov`: symmetric positive definite.
All inputs are finite; a program needn't handle non-finite values.
Results may differ from a plain program's by a relative error of at most 0.0003.
Values sent between devices are 32-bit elements; how exact they have to be, the bound alone decides.
A program may use at most 64 MiB of HBM per device.

v0:
```python
import functools

import jax
import jax.numpy as jnp
from jax import lax
from jax.experimental import pallas as pl
from jax.experimental.pallas import tpu as pltpu
from jax.sharding import PartitionSpec as P

PANEL = 32


def split(value, parts):
    pieces = []
    for at in range(parts):
        pieces.append(value.astype(jnp.bfloat16))
        if at < parts - 1:
            value = value - pieces[-1].astype(jnp.float32)
    return pieces


PAIRS = {2: ((0, 0), (0, 1), (1, 0)), 3: ((0, 0), (0, 1), (1, 0), (1, 1), (0, 2), (2, 0))}


def dot(left, right, dims, parts):
    lefts, rights = split(left, parts), split(right, parts)
    return lax.dot_general(
        jnp.concatenate([lefts[i] for i, _ in PAIRS[parts]], axis=dims[0]),
        jnp.concatenate([rights[j] for _, j in PAIRS[parts]], axis=dims[1]),
        ((dims[:1], dims[1:]), ((), ())),
        preferred_element_type=jnp.float32,
    )


def product(left, right, parts=2):
    return dot(left, right, (1, 0), parts)


def product_t(left, right, parts=2):
    return dot(left, right, (1, 1), parts)


def gram(left, right):
    return dot(left, right, (0, 0), 3)


def invert_all(mats):
    width = mats[0].shape[0]
    panel = min(PANEL, width)
    lane = lax.broadcasted_iota(jnp.int32, (panel, width), 1)
    row = lax.broadcasted_iota(jnp.int32, (panel, width), 0)
    lane_one = lax.broadcasted_iota(jnp.int32, (1, width), 1)
    full_lane = lax.broadcasted_iota(jnp.int32, (width, width), 1)
    for base in range(0, width, panel):
        olds = [mat[base : base + panel] for mat in mats]
        news = list(olds)
        for step in range(panel):
            column = base + step
            clear = (lane == column) | (row == step)
            for at, now in enumerate(news):
                pivots = jnp.broadcast_to(now[:, column : column + 1], now.shape)
                inverse = 1.0 / pivots[step : step + 1]
                pivot_row = jnp.where(lane_one == column, 1.0, now[step : step + 1]) * inverse
                factors = jnp.where(row == step, -1.0, pivots)
                news[at] = jnp.where(clear, 0.0, now) - factors * pivot_row
        inside = (full_lane >= base) & (full_lane < base + panel)
        inside_panel = (lane >= base) & (lane < base + panel)
        for at, mat in enumerate(mats):
            signed = jnp.where(lane < base, -olds[at], olds[at])
            signed = jnp.where(inside_panel, 0.0, signed)
            cleared = jnp.where(inside, 0.0, mat)
            parts = [news[at]]
            if base:
                parts.insert(0, cleared[:base])
            if base + panel < width:
                parts.append(cleared[base + panel :])
            cleared = jnp.concatenate(parts, axis=0)
            mats[at] = cleared - gram(signed, news[at])
    return mats


def combine(later, earlier):
    late_gain, late_mean, late_cov = later
    early_gain, early_mean, early_cov = earlier
    width = late_gain.shape[0]
    half = product(early_gain, late_cov)
    down = product_t(jnp.concatenate([half, late_mean], axis=0), early_gain)
    return product(early_gain, late_gain), down[width:] + early_mean, down[:width] + early_cov


def apply(state, elem):
    mean, cov = state
    gain, offset, resid = elem
    width = gain.shape[0]
    half = product(gain, cov)
    down = product_t(jnp.concatenate([half, mean], axis=0), gain)
    return down[width:] + offset, down[:width] + resid


def choose(flag, first, second):
    return tuple(jnp.where(flag, a, b) for a, b in zip(first, second))


def keep(ref, elem):
    width = ref.shape[1]
    ref[:width], ref[2 * width :], ref[width : 2 * width] = elem


def take(ref):
    width = ref.shape[1]
    return ref[:width], ref[2 * width :], ref[width : 2 * width]


def kernel(
    sizes, mean_ref, cov_ref, noise_ref, reached, held, gains, send, recv, send_sem, recv_sem
):
    steps, width = mean_ref.shape
    levels = []
    for axis in ("narrow", "wide"):
        place = lax.axis_index(axis)
        bit = 1
        while bit < sizes[axis]:
            later = (place // bit) % 2
            levels.append((axis, place + bit - 2 * bit * later, later == 1))
            bit *= 2
        assert bit == sizes[axis]
    if levels:
        barrier = pltpu.get_barrier_semaphore()
        for axis, partner, _ in levels:
            pl.semaphore_signal(
                barrier, inc=1, device_id={axis: partner}, device_id_type=pl.DeviceIdType.MESH
            )

    noise = noise_ref[...]
    inverses = invert_all([cov_ref[t] + noise for t in range(steps)])
    final = (lax.axis_index("wide") == sizes["wide"] - 1) & (
        lax.axis_index("narrow") == sizes["narrow"] - 1
    )
    for t in range(steps):
        gain = product(cov_ref[t], inverses[t], 3)
        if t == steps - 1:
            gain = jnp.where(final, 0.0, gain)
        resid = product(gain, noise)
        if t == steps - 1:
            resid = jnp.where(final, cov_ref[t], resid)
        mean = jnp.broadcast_to(mean_ref[t : t + 1, :], (8, width))
        gains[t] = gain
        keep(held.at[t], (gain, mean - product_t(mean, gain, 3), resid))

    def scan(first, last):
        if last - first == 1:
            return take(held.at[first]), lambda: None
        middle = (first + last) // 2
        late, late_rest = scan(middle, last)
        early, early_rest = scan(first, middle)
        whole = combine(late, early)

        def rest():
            late_rest()
            early_rest()
            keep(held.at[middle], late)
            for t in range(first + 1, middle):
                keep(held.at[t], combine(take(held.at[middle]), take(held.at[t])))
            keep(held.at[first], whole)

        return whole, rest

    total, rest = scan(0, steps)

    eye = (
        lax.broadcasted_iota(jnp.int32, (width, width), 0)
        == lax.broadcasted_iota(jnp.int32, (width, width), 1)
    ).astype(jnp.float32)
    incoming = None
    copies = []

    def post(at, part, rows):
        axis, partner, _ = levels[at]
        copy = pltpu.make_async_remote_copy(
            src_ref=send.at[at, rows],
            dst_ref=recv.at[at, rows],
            send_sem=send_sem.at[at, part],
            recv_sem=recv_sem.at[at, part],
            device_id={axis: partner},
            device_id_type=pl.DeviceIdType.MESH,
        )
        copy.start()
        copies.append(copy)
        return copy

    def post_gain(at, gain):
        send[at, :width] = gain
        return post(at, 0, pl.ds(0, width))

    def post_state(at, state):
        send[at, 2 * width :], send[at, width : 2 * width] = state
        return post(at, 1, pl.ds(width, width + 8))

    last = len(levels) - 1
    gain_copy = state_copy = other = None
    if levels:
        pl.semaphore_wait(barrier, len(levels))
        if last > 0:
            gain_copy = post_gain(0, total[0])
        state_copy = post_state(0, total[1:])
    rest()
    for at, (_, _, later) in enumerate(levels):
        if at < last:
            gain_copy.wait_recv()
            other_gain = recv[at, :width]
            late_gain = jnp.where(later, total[0], other_gain)
            early_gain = jnp.where(later, other_gain, total[0])
            if at < last - 1:
                joined_gain = product(early_gain, late_gain)
                gain_copy = post_gain(at + 1, joined_gain)
        state_copy.wait_recv()
        other_state = (recv[at, 2 * width :], recv[at, width : 2 * width])
        if at < last:
            late_state = choose(later, total[1:], other_state)
            early_state = choose(later, other_state, total[1:])
            joined = apply(late_state, (early_gain,) + early_state)
            state_copy = post_state(at + 1, joined)
            total = (joined_gain if at < last - 1 else None,) + joined
            other = (other_gain,) + other_state
            if incoming is None:
                blank = (eye, jnp.zeros((8, width), jnp.float32), jnp.zeros_like(eye))
                incoming = choose(later, blank, other)
            else:
                incoming = choose(later, incoming, combine(other, incoming))
    zero_state = (jnp.zeros((8, width), jnp.float32), jnp.zeros((width, width), jnp.float32))
    if not levels:
        state = zero_state
    elif incoming is None:
        state = choose(later, zero_state, other_state)
    else:
        state = choose(later, incoming[1:], apply(other_state, incoming))
    reached[width:], reached[:width] = state
    for copy in copies:
        copy.wait_send()


def finish(sizes, reached, held, gains, out_mean, out_cov, out_inc):
    steps, width = out_mean.shape
    final = (lax.axis_index("wide") == sizes["wide"] - 1) & (
        lax.axis_index("narrow") == sizes["narrow"] - 1
    )
    eye = (
        lax.broadcasted_iota(jnp.int32, (width, width), 0)
        == lax.broadcasted_iota(jnp.int32, (width, width), 1)
    ).astype(jnp.float32)
    state = reached[width:], reached[:width]
    results = [apply(state, take(held.at[t])) for t in range(steps)]
    ones = jnp.ones((8, width), jnp.float32)
    for t in range(steps):
        mean, cov = results[t]
        next_mean, next_cov = results[t + 1] if t < steps - 1 else state
        out_mean[t : t + 1, :] = mean[:1]
        out_cov[t] = cov
        change = next_mean - mean
        spread = product_t(ones, eye * (next_cov + cov) - 2.0 * (next_cov * gains[t]))
        increment = change * change + spread
        if t == steps - 1:
            increment = jnp.where(final, 0.0, increment)
        out_inc[t : t + 1, :] = increment[:1]


def per_device(sizes, filt_mean, filtered_covariance, noise_cov):
    steps, width = filt_mean.shape
    count = sum(size.bit_length() - 1 for size in sizes.values())
    slots = max(count, 1)
    block = (slots, 2 * width + 8, width)
    params = dict(collective_id=0, has_side_effects=True) if count else {}
    vmem = pl.BlockSpec(memory_space=pltpu.VMEM)
    parts = pl.pallas_call(
        functools.partial(kernel, sizes),
        out_shape=(
            jax.ShapeDtypeStruct((width + 8, width), jnp.float32),
            jax.ShapeDtypeStruct((steps,) + block[1:], jnp.float32),
            jax.ShapeDtypeStruct((steps, width, width), jnp.float32),
        ),
        in_specs=[vmem] * 3,
        out_specs=(vmem,) * 3,
        scratch_shapes=[
            pltpu.VMEM(block, jnp.float32),
            pltpu.VMEM(block, jnp.float32),
            pltpu.SemaphoreType.DMA((slots, 2)),
            pltpu.SemaphoreType.DMA((slots, 2)),
        ],
        compiler_params=pltpu.CompilerParams(vmem_limit_bytes=24 << 20, **params),
    )(filt_mean, filtered_covariance, noise_cov)
    return pl.pallas_call(
        functools.partial(finish, sizes),
        out_shape=(
            jax.ShapeDtypeStruct((steps, width), jnp.float32),
            jax.ShapeDtypeStruct((steps, width, width), jnp.float32),
            jax.ShapeDtypeStruct((steps, width), jnp.float32),
        ),
        in_specs=[vmem] * 3,
        out_specs=(vmem,) * 3,
        compiler_params=pltpu.CompilerParams(vmem_limit_bytes=24 << 20),
    )(*parts)


def solution(mesh):
    sizes = {axis: mesh.shape[axis] for axis in ("wide", "narrow")}
    return jax.shard_map(
        functools.partial(per_device, sizes),
        mesh=mesh,
        in_specs=(P(("wide", "narrow"), None), P(("wide", "narrow"), None, None), P()),
        out_specs=(
            P(("wide", "narrow"), None),
            P(("wide", "narrow"), None, None),
            P(("wide", "narrow"), None),
        ),
        check_vma=False,
    )
```

profile of v0, /device:TPU:0, one launch (start us, length us, event | category | flops | bytes accessed | tf_op | source)
XLA Modules:
  0.0 41.6 jit_solution(14197801482631549062)
XLA Ops:
  0.6 0.0 copy-start
  0.6 0.9 %copy-done = f32[4,128,128]{2,1,0:T(8,128)S(1)} copy-done((f32[4,128,128]{2,1,0:T(8,128)S(1)}, f32[4,128,128]{2,1,0:T(8,128)}, u32[]{:S(2)}) %copy-start) | copy-done | bytes 262168
  1.6 0.0 copy-start.1
  1.6 0.8 %copy-done.1 = f32[128,128]{1,0:T(8,128)S(1)} copy-done((f32[128,128]{1,0:T(8,128)S(1)}, f32[128,128]{1,0:T(8,128)}, u32[]{:S(2)}) %copy-start.1) | copy-done | bytes 65560
  2.4 0.0 copy-start.2
  2.4 0.7 %copy-done.2 = f32[4,128]{1,0:T(4,128)S(1)} copy-done((f32[4,128]{1,0:T(4,128)S(1)}, f32[4,128]{1,0:T(4,128)}, u32[]{:S(2)}) %copy-start.2) | copy-done | bytes 2072
  3.1 36.9 %shard_map.58 = (f32[136,128]{1,0:T(8,128)S(1)}, f32[4,264,128]{2,1,0:T(8,128)S(1)}, f32[4,128,128]{2,1,0:T(8,128)S(1)}) custom-call(f32[4,128]{1,0:T(4,128)S(1)} %copy-done.2, f32[4,128,128]{2,1,0:T(8,128)S(1)} %copy-done, f32[128,128]{1,0:T(8,128)S(1)} %copy-done.1), custom_call_target="tpu_custom_call" | custom-call | tf_op jit(solution)/shard_map/pallas_call | solution.py:274
  40.0 1.6 %shard_map.59 = (f32[4,128]{1,0:T(4,128)}, f32[4,128,128]{2,1,0:T(8,128)}, f32[4,128]{1,0:T(4,128)}) custom-call(f32[136,128]{1,0:T(8,128)S(1)} %get-tuple-element.6.reached, f32[4,264,128]{2,1,0:T(8,128)S(1)} %get-tuple-element.7.held, f32[4,128,128]{2,1,0:T(8,128)S(1)} %get-tuple-element.8.gains), custom_call_target="tpu_custom_call" | custom-call | tf_op jit(solution)/shard_map/pallas_call | solution.py:291
Async XLA Ops:
  0.6 1.0 %copy-start = (f32[4,128,128]{2,1,0:T(8,128)S(1)}, f32[4,128,128]{2,1,0:T(8,128)}, u32[]{:S(2)}) copy-start(f32[4,128,128]{2,1,0:T(8,128)} %cov_ref.1) | copy-start | bytes 786436
  1.6 0.8 %copy-start.1 = (f32[128,128]{1,0:T(8,128)S(1)}, f32[128,128]{1,0:T(8,128)}, u32[]{:S(2)}) copy-start(f32[128,128]{1,0:T(8,128)} %noise_ref.1) | copy-start | bytes 196612
  2.4 0.7 %copy-start.2 = (f32[4,128]{1,0:T(4,128)S(1)}, f32[4,128]{1,0:T(4,128)}, u32[]{:S(2)}) copy-start(f32[4,128]{1,0:T(4,128)} %mean_ref.1) | copy-start | bytes 6148
where the time goes:
time: 41.8 us; the launch traced here: 41.6 us
  Pallas kernels  38.5 us (92%)
  local copies, waits for them, and re-layouts  2.46 us (6%)
  between operations  0.65 us (2%)
    pallas_call x1, Pallas kernels, per_device(): pl.pallas_call(functools.partial(kernel, sizes), out_shape=(jax.ShapeDtyp...  36.9 us
    unnamed x6, local copies, waits for them, and re-layouts  2.46 us
    pallas_call x1, Pallas kernels, per_device(): pl.pallas_call(functools.partial(finish, sizes), out_shape=(jax.ShapeDtyp...  1.58 us

commit v1 on v0

--- a/solution.py
+++ b/solution.py
@@ -7,7 +7,9 @@
 from jax.experimental.pallas import tpu as pltpu
 from jax.sharding import PartitionSpec as P
 
-PANEL = 32
+PANEL = 16
+SUB = 8
+SCALE = 0.0625
 
 
 def split(value, parts):
@@ -45,37 +47,56 @@
 
 
 def invert_all(mats):
+    mats=list(mats)
     width = mats[0].shape[0]
-    panel = min(PANEL, width)
-    lane = lax.broadcasted_iota(jnp.int32, (panel, width), 1)
-    row = lax.broadcasted_iota(jnp.int32, (panel, width), 0)
-    lane_one = lax.broadcasted_iota(jnp.int32, (1, width), 1)
-    full_lane = lax.broadcasted_iota(jnp.int32, (width, width), 1)
+    panel, sub = min(PANEL, width), min(SUB, width)
+    lane = lax.broadcasted_iota(jnp.int32, (sub, width), 1)
+    row = lax.broadcasted_iota(jnp.int32, (sub, width), 0)
+    wide_lane = lax.broadcasted_iota(jnp.int32, (panel, width), 1)
+    wide_row = lax.broadcasted_iota(jnp.int32, (panel, width), 0)
+    count = len(mats)
+    span = lambda v, k: jnp.broadcast_to(v[k : k + 1], v.shape)
+    ones_row = [(row == k).astype(jnp.float32) for k in range(sub)]
     for base in range(0, width, panel):
         olds = [mat[base : base + panel] for mat in mats]
-        news = list(olds)
-        for step in range(panel):
-            column = base + step
-            clear = (lane == column) | (row == step)
-            for at, now in enumerate(news):
-                pivots = jnp.broadcast_to(now[:, column : column + 1], now.shape)
-                inverse = 1.0 / pivots[step : step + 1]
-                pivot_row = jnp.where(lane_one == column, 1.0, now[step : step + 1]) * inverse
-                factors = jnp.where(row == step, -1.0, pivots)
-                news[at] = jnp.where(clear, 0.0, now) - factors * pivot_row
-        inside = (full_lane >= base) & (full_lane < base + panel)
-        inside_panel = (lane >= base) & (lane < base + panel)
+        news = [[old[at : at + sub] for at in range(0, panel, sub)] for old in olds]
+        for s in range(panel // sub):
+            off = base + s * sub
+            spread = lambda v: [jnp.broadcast_to(v[:, off + j : off + j + 1], v.shape) for j in range(sub)]
+            cols = [spread(new[s]) for new in news]
+            others = [[spread(new[r]) if r != s else None for r in range(panel // sub)] for new in news]
+            for k in range(sub):
+                unit = (lane == off + k).astype(jnp.float32)
+                for at in range(count):
+                    col = cols[at]
+                    inverse = 1.0 / span(col[k], k)
+                    factors = (col[k] - ones_row[k]) * inverse
+                    new = news[at][s]
+                    news[at][s] = new - factors * (span(new, k) + unit)
+                    for j in range(k + 1, sub):
+                        col[j] = col[j] - factors * span(col[j], k)
+            units = (lane == off + row).astype(jnp.float32)
+            for at in range(count):
+                filled = news[at][s] + units
+                rows = [span(filled, j) for j in range(sub)]
+                for r in range(panel // sub):
+                    if r != s:
+                        terms = [others[at][r][j] * rows[j] for j in range(sub)]
+                        while len(terms) > 1:
+                            terms = [a + b for a, b in zip(terms[::2], terms[1::2])]
+                        news[at][r] = news[at][r] - terms[0]
+        inside = (wide_lane >= base) & (wide_lane < base + panel)
+        eye = (wide_lane == base + wide_row).astype(jnp.float32)
         for at, mat in enumerate(mats):
-            signed = jnp.where(lane < base, -olds[at], olds[at])
-            signed = jnp.where(inside_panel, 0.0, signed)
-            cleared = jnp.where(inside, 0.0, mat)
-            parts = [news[at]]
+            signed = jnp.where(wide_lane < base, -olds[at], olds[at])
+            signed = jnp.where(inside, 0.0, signed)
+            new = jnp.concatenate(news[at], axis=0)
+            pieces = [new]
             if base:
-                parts.insert(0, cleared[:base])
+                pieces.insert(0, mat[:base])
             if base + panel < width:
-                parts.append(cleared[base + panel :])
-            cleared = jnp.concatenate(parts, axis=0)
-            mats[at] = cleared - gram(signed, news[at])
+                pieces.append(mat[base + panel :])
+            mats[at] = jnp.concatenate(pieces, axis=0) - gram(signed, new + eye)
     return mats
 
 
@@ -112,8 +133,17 @@
 
 
 def kernel(
-    sizes, mean_ref, cov_ref, noise_ref, reached, held, gains, send, recv, send_sem, recv_sem
+    sizes, mean_hbm, cov_hbm, noise_hbm, reached, held, gains,
+    mean_ref, cov_ref, noise_ref, load_sem, send, recv, send_sem, recv_sem
 ):
+    loads = [
+        pltpu.make_async_copy(source, target, load_sem.at[at])
+        for at, (source, target) in enumerate(
+            ((noise_hbm, noise_ref), (cov_hbm, cov_ref), (mean_hbm, mean_ref))
+        )
+    ]
+    for load in loads:
+        load.start()
     steps, width = mean_ref.shape
     levels = []
     for axis in ("narrow", "wide"):
@@ -131,8 +161,12 @@
                 barrier, inc=1, device_id={axis: partner}, device_id_type=pl.DeviceIdType.MESH
             )
 
+    for load in loads:
+        load.wait()
     noise = noise_ref[...]
-    inverses = invert_all([cov_ref[t] + noise for t in range(steps)])
+    inverses = [
+        mat * SCALE for mat in invert_all([(cov_ref[t] + noise) * SCALE for t in range(steps)])
+    ]
     final = (lax.axis_index("wide") == sizes["wide"] - 1) & (
         lax.axis_index("narrow") == sizes["narrow"] - 1
     )
@@ -278,9 +312,13 @@
             jax.ShapeDtypeStruct((steps,) + block[1:], jnp.float32),
             jax.ShapeDtypeStruct((steps, width, width), jnp.float32),
         ),
-        in_specs=[vmem] * 3,
+        in_specs=[pl.BlockSpec(memory_space=pltpu.HBM)] * 3,
         out_specs=(vmem,) * 3,
         scratch_shapes=[
+            pltpu.VMEM((steps, width), jnp.float32),
+            pltpu.VMEM((steps, width, width), jnp.float32),
+            pltpu.VMEM((width, width), jnp.float32),
+            pltpu.SemaphoreType.DMA((3,)),
             pltpu.VMEM(block, jnp.float32),
             pltpu.VMEM(block, jnp.float32),
             pltpu.SemaphoreType.DMA((slots, 2)),

time: 41.8 us -> 35.1 us (0.84)
  Pallas kernels: 38.5 us -> 31.8 us
    pallas_call x1, Pallas kernels: 36.9 us -> 30.2 us  [per_device(): pl.pallas_call(functools.partial(kernel, sizes), out_shape=(jax.ShapeDtyp...]
where the time goes in v1:
time: 35.1 us; the launch traced here: 34.9 us
  Pallas kernels  31.8 us (91%)
  local copies, waits for them, and re-layouts  2.46 us (7%)
  between operations  0.65 us (2%)
    pallas_call x1, Pallas kernels, per_device(): pl.pallas_call(functools.partial(kernel, sizes), out_shape=(jax.ShapeDtyp...  30.2 us
    unnamed x6, local copies, waits for them, and re-layouts  2.46 us
    pallas_call x1, Pallas kernels, per_device(): pl.pallas_call(functools.partial(finish, sizes), out_shape=(jax.ShapeDtyp...  1.58 us

profile of v1, /device:TPU:0, one launch (start us, length us, event | category | flops | bytes accessed | tf_op | source)
XLA Modules:
  0.0 34.9 jit_solution(5063009135635783870)
XLA Ops:
  0.6 0.0 copy-start
  0.6 0.9 %copy-done = f32[4,128,128]{2,1,0:T(8,128)S(1)} copy-done((f32[4,128,128]{2,1,0:T(8,128)S(1)}, f32[4,128,128]{2,1,0:T(8,128)}, u32[]{:S(2)}) %copy-start) | copy-done | bytes 262168
  1.6 0.0 copy-start.1
  1.6 0.8 %copy-done.1 = f32[128,128]{1,0:T(8,128)S(1)} copy-done((f32[128,128]{1,0:T(8,128)S(1)}, f32[128,128]{1,0:T(8,128)}, u32[]{:S(2)}) %copy-start.1) | copy-done | bytes 65560
  2.4 0.0 copy-start.2
  2.4 0.7 %copy-done.2 = f32[4,128]{1,0:T(4,128)S(1)} copy-done((f32[4,128]{1,0:T(4,128)S(1)}, f32[4,128]{1,0:T(4,128)}, u32[]{:S(2)}) %copy-start.2) | copy-done | bytes 2072
  3.1 30.2 %shard_map.58 = (f32[136,128]{1,0:T(8,128)S(1)}, f32[4,264,128]{2,1,0:T(8,128)S(1)}, f32[4,128,128]{2,1,0:T(8,128)S(1)}) custom-call(f32[4,128]{1,0:T(4,128)S(1)} %copy-done.2, f32[4,128,128]{2,1,0:T(8,128)S(1)} %copy-done, f32[128,128]{1,0:T(8,128)S(1)} %copy-done.1), custom_call_target="tpu_custom_call" | custom-call | tf_op jit(solution)/shard_map/pallas_call | solution.py:308
  33.3 1.6 %shard_map.59 = (f32[4,128]{1,0:T(4,128)}, f32[4,128,128]{2,1,0:T(8,128)}, f32[4,128]{1,0:T(4,128)}) custom-call(f32[136,128]{1,0:T(8,128)S(1)} %get-tuple-element.6.reached, f32[4,264,128]{2,1,0:T(8,128)S(1)} %get-tuple-element.7.held, f32[4,128,128]{2,1,0:T(8,128)S(1)} %get-tuple-element.8.gains), custom_call_target="tpu_custom_call" | custom-call | tf_op jit(solution)/shard_map/pallas_call | solution.py:329
Async XLA Ops:
  0.6 1.0 %copy-start = (f32[4,128,128]{2,1,0:T(8,128)S(1)}, f32[4,128,128]{2,1,0:T(8,128)}, u32[]{:S(2)}) copy-start(f32[4,128,128]{2,1,0:T(8,128)} %cov_hbm.1) | copy-start | bytes 786436
  1.6 0.8 %copy-start.1 = (f32[128,128]{1,0:T(8,128)S(1)}, f32[128,128]{1,0:T(8,128)}, u32[]{:S(2)}) copy-start(f32[128,128]{1,0:T(8,128)} %noise_hbm.1) | copy-start | bytes 196612
  2.4 0.7 %copy-start.2 = (f32[4,128]{1,0:T(4,128)S(1)}, f32[4,128]{1,0:T(4,128)}, u32[]{:S(2)}) copy-start(f32[4,128]{1,0:T(4,128)} %mean_hbm.1) | copy-start | bytes 6148

commit v2 on v1

--- a/solution.py
+++ b/solution.py
@@ -325,7 +325,12 @@
             pltpu.SemaphoreType.DMA((slots, 2)),
         ],
         compiler_params=pltpu.CompilerParams(vmem_limit_bytes=24 << 20, **params),
-    )(filt_mean, filtered_covariance, noise_cov)
+    )(
+        *(
+            pltpu.with_memory_space_constraint(value, pltpu.HBM)
+            for value in (filt_mean, filtered_covariance, noise_cov)
+        )
+    )
     return pl.pallas_call(
         functools.partial(finish, sizes),
         out_shape=(

time: 35.1 us -> 33.5 us (0.954)
  local copies, waits for them, and re-layouts: 2.46 us -> 0 us
  Pallas kernels: 31.8 us -> 32.7 us
    unnamed x6 -> x0, local copies, waits for them, and re-layouts: 2.46 us -> none
    pallas_call x1, Pallas kernels: 30.2 us -> 31.1 us  [per_device(): pl.pallas_call(functools.partial(kernel, sizes), out_shape=(jax.ShapeDtyp...]
where the time goes in v2:
time: 33.5 us; the launch traced here: 33.3 us
  Pallas kernels  32.7 us (98%)
  between operations  0.64 us (2%)
    pallas_call x1, Pallas kernels, per_device(): pl.pallas_call(functools.partial(kernel, sizes), out_shape=(jax.ShapeDtyp...  31.1 us
    pallas_call x1, Pallas kernels, per_device(): pl.pallas_call(functools.partial(finish, sizes), out_shape=(jax.ShapeDtyp...  1.58 us

profile of v2, /device:TPU:0, one launch (start us, length us, event | category | flops | bytes accessed | tf_op | source)
XLA Modules:
  0.0 33.3 jit_solution(3495035011557705673)
XLA Ops:
  0.6 31.1 %shard_map.58 = (f32[136,128]{1,0:T(8,128)S(1)}, f32[4,264,128]{2,1,0:T(8,128)S(1)}, f32[4,128,128]{2,1,0:T(8,128)S(1)}) custom-call(f32[4,128]{1,0:T(4,128)} %mean_hbm.1, f32[4,128,128]{2,1,0:T(8,128)} %cov_hbm.1, f32[128,128]{1,0:T(8,128)} %noise_hbm.1), custom_call_target="tpu_custom_call" | custom-call | tf_op jit(solution)/shard_map/pallas_call | solution.py:308
  31.7 1.6 %shard_map.59 = (f32[4,128]{1,0:T(4,128)}, f32[4,128,128]{2,1,0:T(8,128)}, f32[4,128]{1,0:T(4,128)}) custom-call(f32[136,128]{1,0:T(8,128)S(1)} %get-tuple-element.6.reached, f32[4,264,128]{2,1,0:T(8,128)S(1)} %get-tuple-element.7.held, f32[4,128,128]{2,1,0:T(8,128)S(1)} %get-tuple-element.8.gains), custom_call_target="tpu_custom_call" | custom-call | tf_op jit(solution)/shard_map/pallas_call | solution.py:334
